TPU v7x, 128 devices: a whole 4x4x4 slice. The times are simulated.
128 devices in a mesh: packs: 8 (over x, core), seq: 16 (over y, z).
Axes of the slice: x: 4, y: 4, z: 4, core: 2. Of those that a mesh axis runs over, the one named last changes fastest.
Arguments:
- queries: bfloat16 [16384, 8192], P(('packs', 'seq')), parts along dimension 0, may hold values from -12 to 12
- keys: bfloat16 [16384, 1024], P(('packs', 'seq')), parts along dimension 0, may hold values from -6 to 6
- values: bfloat16 [16384, 1024], P(('packs', 'seq')), parts along dimension 0, may hold values from -6 to 6
- outputs: bfloat16 [16384, 8192], P(('packs', 'seq')), parts along dimension 0, may hold values from -6 to 6
- grad_out: bfloat16 [16384, 8192], P(('packs', 'seq')), parts along dimension 0, may hold values from -4 to 4
- lse_saved: float32 [16384, 64], P(('packs', 'seq')), parts along dimension 0, may hold values from -40 to 40
- doc_lengths: int32 [64], P('packs'), parts along dimension 0, may hold values from 1 to 1024, as said below
Outputs:
- grad_queries: bfloat16 [16384, 8192], P(('packs', 'seq')), parts along dimension 0
- grad_keys: bfloat16 [16384, 1024], P(('packs', 'seq')), parts along dimension 0
- grad_values: bfloat16 [16384, 1024], P(('packs', 'seq')), parts along dimension 0
There are 8 independent parts, one for each index of `packs`. A program takes and returns all parts, laid end to end along the dimension named above; each array names one. Nothing has to cross between parts.
Inputs may be any that keep to these rules, and one draw needn't show every extreme that they name: `doc_lengths`: positive lengths summing to 2048; one document has exactly 1024 tokens.
All inputs are finite; a program needn't handle non-finite values.
Results may differ from a plain program's by a relative error of at most 0.0049.
Values may be sent and summed in bfloat16 or wider, within the bound.
A program may use at most 64 MiB of HBM per device.

v0:
```python
import jax
import jax.numpy as jnp
from jax import lax
from jax.sharding import PartitionSpec as P

HEADS = 64
KVH = 8
HDIM = 128


def segment_ids(doc_lengths, total):
    boundary = jnp.cumsum(doc_lengths)
    position = jnp.arange(total, dtype=jnp.int32)
    return jnp.sum((position[:, None] >= boundary[None, :]).astype(jnp.int32), axis=1)


def left_dot(first, second):
    return lax.dot_general(
        first, second, (((0,), (0,)), ((), ())), preferred_element_type=jnp.float32
    )


def right_dot(first, second):
    return lax.dot_general(
        first, second, (((1,), (1,)), ((), ())), preferred_element_type=jnp.float32
    )


def block_terms(
    query_blk,
    gout_blk,
    lse_blk,
    delta_blk,
    query_seg,
    query_pos,
    key_blk,
    value_blk,
    key_seg,
    key_pos,
    scale,
):
    scores = right_dot(query_blk, key_blk) * scale
    visible = (key_pos[None, :] <= query_pos[:, None]) & (key_seg[None, :] == query_seg[:, None])
    attn_prob = jnp.where(visible, jnp.exp(scores - lse_blk[:, None]), 0.0)
    grad_prob = right_dot(gout_blk, value_blk)
    grad_score = (attn_prob * (grad_prob - delta_blk[:, None])).astype(jnp.bfloat16)
    prob_half = attn_prob.astype(jnp.bfloat16)
    grad_query = jnp.dot(grad_score, key_blk, preferred_element_type=jnp.float32) * scale
    grad_key = left_dot(grad_score, query_blk) * scale
    grad_value = left_dot(prob_half, gout_blk)
    return (grad_query, grad_key, grad_value)


def shards(queries, keys, values, outputs, grad_out, lse_saved, doc_lengths):
    seq_size = lax.axis_size("seq")
    local_rows = queries.shape[0]
    total = local_rows * seq_size
    head_dim = HDIM
    heads_here = HEADS // seq_size
    share_count = seq_size // KVH
    scale = 1.0 / head_dim**0.5

    def to_slots(array):
        return array.reshape(local_rows, seq_size, heads_here * head_dim)

    query_heads, out_heads, gout_heads = (
        lax.all_to_all(to_slots(queries), "seq", split_axis=1, concat_axis=0, tiled=True),
        lax.all_to_all(to_slots(outputs), "seq", split_axis=1, concat_axis=0, tiled=True),
        lax.all_to_all(to_slots(grad_out), "seq", split_axis=1, concat_axis=0, tiled=True),
    )
    lse_heads = lax.all_to_all(
        lse_saved.reshape(local_rows, seq_size, heads_here),
        "seq",
        split_axis=1,
        concat_axis=0,
        tiled=True,
    )
    out_heads = out_heads.reshape(total, heads_here, head_dim)
    gout_heads = gout_heads.reshape(total, heads_here, head_dim)
    delta_heads = jnp.einsum(
        "thd,thd->th", out_heads, gout_heads, preferred_element_type=jnp.float32
    )
    query_heads = query_heads.reshape(total, heads_here, head_dim)
    lse_heads = lse_heads.reshape(total, heads_here)
    key_slots = jnp.repeat(keys.reshape(local_rows, KVH, head_dim), share_count, axis=1)
    value_slots = jnp.repeat(values.reshape(local_rows, KVH, head_dim), share_count, axis=1)
    key_heads, value_heads = (
        lax.all_to_all(key_slots, "seq", split_axis=1, concat_axis=0, tiled=True),
        lax.all_to_all(value_slots, "seq", split_axis=1, concat_axis=0, tiled=True),
    )
    key_heads = key_heads.reshape(total, head_dim)
    value_heads = value_heads.reshape(total, head_dim)
    segment = segment_ids(doc_lengths, total)
    position = jnp.arange(total, dtype=jnp.int32)
    block = min(512, total)
    num_blocks = total // block

    def step(carry, index):
        grad_q_all, grad_k_acc, grad_v_acc = carry
        head = index // num_blocks
        start = index % num_blocks * block
        query_blk = lax.dynamic_slice(query_heads, (start, head, 0), (block, 1, head_dim)).reshape(
            block, head_dim
        )
        gout_blk = lax.dynamic_slice(gout_heads, (start, head, 0), (block, 1, head_dim)).reshape(
            block, head_dim
        )
        lse_blk = lax.dynamic_slice(lse_heads, (start, head), (block, 1)).reshape(block)
        delta_blk = lax.dynamic_slice(delta_heads, (start, head), (block, 1)).reshape(block)
        query_seg = lax.dynamic_slice_in_dim(segment, start, block)
        query_pos = lax.dynamic_slice_in_dim(position, start, block)
        grad_query, grad_key, grad_value = block_terms(
            query_blk,
            gout_blk,
            lse_blk,
            delta_blk,
            query_seg,
            query_pos,
            key_heads,
            value_heads,
            segment,
            position,
            scale,
        )
        grad_k_acc = grad_k_acc + grad_key
        grad_v_acc = grad_v_acc + grad_value
        grad_q_all = lax.dynamic_update_slice(
            grad_q_all,
            grad_query.astype(jnp.bfloat16).reshape(block, 1, head_dim),
            (start, head, 0),
        )
        return ((grad_q_all, grad_k_acc, grad_v_acc), None)

    start_carry = (
        jnp.zeros((total, heads_here, head_dim), jnp.bfloat16),
        jnp.zeros((total, head_dim), jnp.float32),
        jnp.zeros((total, head_dim), jnp.float32),
    )
    final_carry, unused = lax.scan(
        step, start_carry, jnp.arange(heads_here * num_blocks, dtype=jnp.int32)
    )
    grad_q_all, grad_k_acc, grad_v_acc = final_carry
    grad_queries = lax.all_to_all(
        grad_q_all.reshape(total, 1, heads_here * head_dim),
        "seq",
        split_axis=0,
        concat_axis=1,
        tiled=True,
    )
    grad_queries = grad_queries.reshape(local_rows, HEADS * head_dim)
    key_back, value_back = (
        lax.all_to_all(
            grad_k_acc.reshape(total, 1, head_dim), "seq", split_axis=0, concat_axis=1, tiled=True
        ),
        lax.all_to_all(
            grad_v_acc.reshape(total, 1, head_dim), "seq", split_axis=0, concat_axis=1, tiled=True
        ),
    )
    grad_keys = (
        jnp.sum(key_back.reshape(local_rows, KVH, share_count, head_dim), axis=2)
        .reshape(local_rows, KVH * head_dim)
        .astype(jnp.bfloat16)
    )
    grad_values = (
        jnp.sum(value_back.reshape(local_rows, KVH, share_count, head_dim), axis=2)
        .reshape(local_rows, KVH * head_dim)
        .astype(jnp.bfloat16)
    )
    return (grad_queries, grad_keys, grad_values)


def solution(mesh):
    placed = (
        P(("packs", "seq"), None),
        P(("packs", "seq"), None),
        P(("packs", "seq"), None),
        P(("packs", "seq"), None),
        P(("packs", "seq"), None),
        P(("packs", "seq"), None),
        P("packs"),
    )
    return jax.shard_map(
        shards,
        mesh=mesh,
        in_specs=placed,
        out_specs=(P(("packs", "seq"), None), P(("packs", "seq"), None), P(("packs", "seq"), None)),
        check_vma=False,
    )
```

profile of v0, /device:TPU:0, one launch (start us, length us, event | category | flops | bytes accessed | tf_op | source)
XLA Modules:
  0.0 481.4 jit_solution(6178511105931249375)
XLA Ops:
  0.7 8.3 %all-to-all-start.2 = ((f32[128,16,4]{0,2,1:T(4,128)}), f32[128,16,4]{0,2,1:T(4,128)S(1)}, u32[]{:S(2)}, u32[]{:S(2)}) async-start(f32[128,16,4]{0,2,1:T(4,128)} %bitcast.141), calls=%async_computation.2 | async-start | bytes 65536 | tf_op jit(solution)/shard_map/all_to_all | solution.py:71
  9.0 7.6 %all-to-all-done.2 = f32[128,16,4]{0,2,1:T(4,128)S(1)} async-done(((f32[128,16,4]{0,2,1:T(4,128)}), f32[128,16,4]{0,2,1:T(4,128)S(1)}, u32[]{:S(2)}, u32[]{:S(2)}) %all-to-all-start.2) | async-done | bytes 32800 | tf_op jit(solution)/shard_map/all_to_all | solution.py:71
  17.5 3.6 all-to-all-start.1
  23.5 7.9 %all-to-all-done.1 = bf16[128,16,128]{2,0,1:T(8,128)(2,1)S(1)} async-done(((bf16[128,16,128]{2,0,1:T(8,128)(2,1)}), bf16[128,16,128]{2,0,1:T(8,128)(2,1)S(1)}, u32[]{:S(2)}, u32[]{:S(2)}) %all-to-all-start.1) | async-done | bytes 524320 | tf_op jit(solution)/shard_map/all_to_all | solution.py:88
  31.4 3.7 all-to-all-start
  35.1 4.1 copy.71
  39.2 23.6 %all-to-all-done = bf16[128,16,512]{0,2,1:T(8,128)(2,1)S(1)} async-done(((bf16[128,16,512]{0,2,1:T(8,128)(2,1)}), bf16[128,16,512]{0,2,1:T(8,128)(2,1)S(1)}, u32[]{:S(2)}, u32[]{:S(2)}) %all-to-all-start) | async-done | bytes 2097184 | tf_op jit(solution)/shard_map/all_to_all | solution.py:67
  64.1 4.4 all-to-all-start.5
  68.6 4.1 copy.68
  72.6 23.6 %all-to-all-done.5 = bf16[128,16,512]{0,2,1:T(8,128)(2,1)} async-done(((bf16[128,16,512]{0,2,1:T(8,128)(2,1)}), bf16[128,16,512]{0,2,1:T(8,128)(2,1)}, u32[]{:S(2)}, u32[]{:S(2)}) %all-to-all-start.5) | async-done | bytes 2097184 | tf_op jit(solution)/shard_map/all_to_all | solution.py:68
  96.3 4.3 all-to-all-start.3
  100.7 27.7 %all-to-all-done.3 = bf16[128,16,512]{0,2,1:T(8,128)(2,1)S(1)} async-done(((bf16[128,16,512]{0,2,1:T(8,128)(2,1)}), bf16[128,16,512]{0,2,1:T(8,128)(2,1)S(1)}, u32[]{:S(2)}, u32[]{:S(2)}) %all-to-all-start.3) | async-done | bytes 2097184 | tf_op jit(solution)/shard_map/all_to_all | solution.py:69
  129.9 4.2 all-to-all-start.4
  134.4 4.3 copy.66
  138.7 4.2 reshape.128
  142.9 4.3 copy.72
  147.2 4.2 reshape.140
  151.4 4.3 copy.69
  155.6 4.1 reshape.135
  159.8 2.9 fusion.16
  164.3 235.0 %while.18 = (s32[]{:T(128)}, bf16[2048,4,128]{0,2,1:T(8,128)(2,1)}, f32[2048,128]{1,0:T(8,128)}, f32[2048,128]{1,0:T(8,128)S(1)}, s32[2048]{0:T(1024)S(1)}, /*in...) while((s32[]{:T(128)}, bf16[2048,4,128]{0,2,1:T(8,128)(2,1)}, ...), condition=%wide.region_3.4_spmd.clone.clone, body=%wide.region_2.3_spmd.clone.clone.sunk | while | flops 1354104832 | bytes 25862684 | solution.py:139
  167.8 2.6 exponential_select_fusion.2
  175.1 2.7 fusion.47
  182.1 2.5 exponential_select_fusion.2
  189.4 3.1 fusion.47
  196.9 2.6 exponential_select_fusion.2
  204.1 3.1 fusion.47
  211.6 2.6 exponential_select_fusion.2
  218.8 3.1 fusion.47
  226.3 2.6 exponential_select_fusion.2
  233.6 3.1 fusion.47
  241.0 2.6 exponential_select_fusion.2
  248.3 3.1 fusion.47
  255.7 2.6 exponential_select_fusion.2
  263.0 3.1 fusion.47
  270.4 2.6 exponential_select_fusion.2
  277.7 3.1 fusion.47
  285.1 2.6 exponential_select_fusion.2
  292.4 3.1 fusion.47
  299.8 2.6 exponential_select_fusion.2
  307.1 3.1 fusion.47
  314.5 2.6 exponential_select_fusion.2
  321.8 3.1 fusion.47
  329.2 2.6 exponential_select_fusion.2
  336.5 3.1 fusion.47
  344.0 2.6 exponential_select_fusion.2
  351.3 3.1 fusion.47
  358.7 2.6 exponential_select_fusion.2
  366.0 3.1 fusion.47
  373.4 2.6 exponential_select_fusion.2
  380.7 3.1 fusion.47
  388.1 2.6 exponential_select_fusion.2
  395.4 3.1 fusion.47
  399.3 21.5 %all_to_all.135 = f32[2048,1,128]{2,1,0:T(1,128)} all-to-all(f32[2048,1,128]{2,1,0:T(1,128)S(1)} %bitcast.123), channel_id=1, replica_groups=mesh['packs'=8,'seq'=16] {'seq'}, dimensions={0} | all-to-all | bytes 2097152 | tf_op jit(solution)/shard_map/all_to_all | solution.py:155
  420.8 4.0 all-to-all-start.7
  425.3 2.9 reduce.2
  428.3 2.9 copy.97
  431.1 2.8 reshape.156
  433.9 4.1 all-to-all-done.7
  438.0 3.7 all-to-all-start.6
  446.8 18.6 %all-to-all-done.6 = bf16[16,2,32768]{2,1,0:T(2,128)(2,1)S(1)} async-done(((bf16[16,2,32768]{2,1,0:T(2,128)(2,1)}), bf16[16,2,32768]{2,1,0:T(2,128)(2,1)S(1)}, u32[]{:S(2)}, u32[]{:S(2)}) %all-to-all-start.6) | async-done | bytes 2097184 | tf_op jit(solution)/shard_map/all_to_all | solution.py:143
  465.5 6.7 %reshape.157 = bf16[2048,1,512]{2,1,0:T(2,128)(2,1)} reshape(bf16[16,2,32768]{2,1,0:T(2,128)(2,1)S(1)} %all-to-all-done.6) | data formatting | bytes 4194304
  472.1 2.8 copy.92
  477.3 4.1 copy.80
  (197 shorter events, 118.1 us)
Async XLA Ops:
  0.6 8.3 %copy-start = (bf16[128,1024]{1,0:T(8,128)(2,1)S(1)}, bf16[128,1024]{1,0:T(8,128)(2,1)}, u32[]{:S(2)}) copy-start(bf16[128,1024]{1,0:T(8,128)(2,1)} %param.10) | copy-start | bytes 786436
  0.6 20.4 %copy-start.5 = (bf16[128,8192]{1,0:T(8,128)(2,1)S(1)}, bf16[128,8192]{1,0:T(8,128)(2,1)}, u32[]{:S(2)}) copy-start(bf16[128,8192]{1,0:T(8,128)(2,1)} %param.9) | copy-start | bytes 6291460
  0.7 15.9 %all-to-all-start.2 = ((f32[128,16,4]{0,2,1:T(4,128)}), f32[128,16,4]{0,2,1:T(4,128)S(1)}, u32[]{:S(2)}, u32[]{:S(2)}) async-start(f32[128,16,4]{0,2,1:T(4,128)} %bitcast.141), calls=%async_computation.2 | async-start | bytes 65536 | tf_op jit(solution)/shard_map/all_to_all | solution.py:71
  17.5 13.9 %all-to-all-start.1 = ((bf16[128,16,128]{2,0,1:T(8,128)(2,1)}), bf16[128,16,128]{2,0,1:T(8,128)(2,1)S(1)}, u32[]{:S(2)}, u32[]{:S(2)}) async-start(bf16[128,16,128]{2,0,1:T(8,128)(2,1)} %bitcast.5), calls=%async_computation.1 | async-start | bytes 1048576 | tf_op jit(solution)/shard_map/all_to_all | solution.py:88
  31.4 31.4 %all-to-all-start = ((bf16[128,16,512]{0,2,1:T(8,128)(2,1)}), bf16[128,16,512]{0,2,1:T(8,128)(2,1)S(1)}, u32[]{:S(2)}, u32[]{:S(2)}) async-start(bf16[128,16,512]{0,2,1:T(8,128)(2,1)} %bitcast.129), calls=%async_computation | async-start | bytes 4194304 | tf_op jit(solution)/shard_map/all_to_all | solution.py:67
  62.8 1.3 copy-start.2
  64.1 32.2 %all-to-all-start.5 = ((bf16[128,16,512]{0,2,1:T(8,128)(2,1)}), bf16[128,16,512]{0,2,1:T(8,128)(2,1)}, u32[]{:S(2)}, u32[]{:S(2)}) async-start(bf16[128,16,512]{0,2,1:T(8,128)(2,1)} %bitcast.130), calls=%async_computation.5 | async-start | bytes 4194304 | tf_op jit(solution)/shard_map/all_to_all | solution.py:68
  96.3 4.4 copy-start.6
  96.3 32.2 %all-to-all-start.3 = ((bf16[128,16,512]{0,2,1:T(8,128)(2,1)}), bf16[128,16,512]{0,2,1:T(8,128)(2,1)S(1)}, u32[]{:S(2)}, u32[]{:S(2)}) async-start(bf16[128,16,512]{0,2,1:T(8,128)(2,1)} %bitcast.131), calls=%async_computation.3 | async-start | bytes 4194304 | tf_op jit(solution)/shard_map/all_to_all | solution.py:69
  100.6 33.5 %copy-start.7 = (s32[8]{0:T(128)S(1)}, s32[8]{0:T(128)}, u32[]{:S(2)}) copy-start(s32[8]{0:T(128)} %param.15) | copy-start | bytes 100
  128.5 1.5 copy-start.3
  129.9 32.8 %all-to-all-start.4 = ((bf16[128,16,128]{2,0,1:T(8,128)(2,1)}), bf16[128,16,128]{2,0,1:T(8,128)(2,1)S(1)}, u32[]{:S(2)}, u32[]{:S(2)}) async-start(bf16[128,16,128]{2,0,1:T(8,128)(2,1)} %bitcast.16), calls=%async_computation.4 | async-start | bytes 1048576 | tf_op jit(solution)/shard_map/all_to_all | solution.py:89
  420.8 4.5 copy-start.4
  420.8 17.2 %all-to-all-start.7 = ((f32[2048,1,128]{2,1,0:T(1,128)}), f32[2048,1,128]{2,1,0:T(1,128)S(1)}, u32[]{:S(2)}, u32[]{:S(2)}) async-start(f32[2048,1,128]{2,1,0:T(1,128)} %bitcast.26), calls=%async_computation.7 | async-start | bytes 2097152 | tf_op jit(solution)/shard_map/all_to_all | solution.py:152
  438.0 27.4 %all-to-all-start.6 = ((bf16[16,2,32768]{2,1,0:T(2,128)(2,1)}), bf16[16,2,32768]{2,1,0:T(2,128)(2,1)S(1)}, u32[]{:S(2)}, u32[]{:S(2)}) async-start(bf16[16,2,32768]{2,1,0:T(2,128)(2,1)} %reshape.156), calls=%async_computation.6 | async-start | bytes 4194304 | tf_op jit(solution)/shard_map/all_to_all | solution.py:143
  477.3 4.1 copy-start.1
where the time goes:
time: 485 us; the launch traced here: 481 us
  matrix products  166 us (34%)
  waiting for transfers between devices  113 us (23%)
  local copies, waits for them, and re-layouts  93.8 us (19%)
  loops' own time  42.5 us (9%)
  starting transfers between devices  36.3 us (7%)
  blocking collectives  21.5 us (4%)
  other arithmetic  7.52 us (2%)
    dot_general x32, matrix products, left_dot(): lax.dot_general(first, second, (((0,), (0,)), ((), ())), preferred_elemen...  83.9 us
    dot_general x32, matrix products, right_dot(): lax.dot_general(first, second, (((1,), (1,)), ((), ())), preferred_elemen...  70.4 us
    another operation x1, loops' own time, shards(): lax.scan(step, start_carry, jnp.arange(heads_here * num_blocks, dtype=jnp...  42.5 us
    unnamed x26, local copies, waits for them, and re-layouts  34.3 us
    all_to_all x1, waiting for transfers between devices, shards(): lax.all_to_all(to_slots(grad_out), 'seq', split_axis=1, concat_axis=0, ti...  27.7 us
    all_to_all x1, waiting for transfers between devices, shards(): lax.all_to_all(to_slots(outputs), 'seq', split_axis=1, concat_axis=0, til...  23.6 us
    all_to_all x1, waiting for transfers between devices, shards(): lax.all_to_all(to_slots(queries), 'seq', split_axis=1, concat_axis=0, til...  23.6 us
    all_to_all x1, blocking collectives, shards(): lax.all_to_all(grad_v_acc.reshape(total, 1, head_dim), 'seq', split_axis=...  21.5 us
  transfers between devices with their start and end apart: 8, of which 7 were waited for; matrix products, arithmetic and copies ran while one was open for 11% of the time, Pallas kernels for 0%

commit v1 on v0

--- a/solution.py
+++ b/solution.py
@@ -6,6 +6,9 @@
 HEADS = 64
 KVH = 8
 HDIM = 128
+do_rates_in = lambda u_in, ax_name: jnp.concatenate(
+    lax.all_to_all(jnp.stack(jnp.split(u_in, lax.psum(1, ax_name), axis=1)), ax_name, 0, 0), axis=0
+)
 
 
 def segment_ids(doc_lengths, total):
@@ -64,7 +67,7 @@
         return array.reshape(local_rows, seq_size, heads_here * head_dim)
 
     query_heads, out_heads, gout_heads = (
-        lax.all_to_all(to_slots(queries), "seq", split_axis=1, concat_axis=0, tiled=True),
+        do_rates_in(to_slots(queries), "seq"),
         lax.all_to_all(to_slots(outputs), "seq", split_axis=1, concat_axis=0, tiled=True),
         lax.all_to_all(to_slots(grad_out), "seq", split_axis=1, concat_axis=0, tiled=True),
     )

time: 485 us -> 494 us (1.019)
  local copies, waits for them, and re-layouts: 93.8 us -> 105 us
  waiting for transfers between devices: 113 us -> 107 us
    unnamed x26 -> x39, local copies, waits for them, and re-layouts: 34.3 us -> 45.1 us
    all_to_all x1, waiting for transfers between devices: 7.56 us -> 0.01 us  [shards(): lax.all_to_all(lse_saved.reshape(local_rows, seq_size, heads_here), 'seq'...]
  transfers between devices with their start and end apart: 8 -> 8, of which waited for: 7 -> 6; matrix products, arithmetic and copies ran while one was open for 11% -> 13% of each run, Pallas kernels for 0% -> 0%
where the time goes in v1:
time: 494 us; the launch traced here: 490 us
  matrix products  166 us (34%)
  waiting for transfers between devices  107 us (22%)
  local copies, waits for them, and re-layouts  105 us (21%)
  loops' own time  42.5 us (9%)
  starting transfers between devices  39.9 us (8%)
  blocking collectives  21.5 us (4%)
  other arithmetic  7.52 us (2%)
    dot_general x32, matrix products, left_dot(): lax.dot_general(first, second, (((0,), (0,)), ((), ())), preferred_elemen...  84 us
    dot_general x32, matrix products, right_dot(): lax.dot_general(first, second, (((1,), (1,)), ((), ())), preferred_elemen...  70.2 us
    unnamed x39, local copies, waits for them, and re-layouts  45.1 us
    another operation x1, loops' own time, shards(): lax.scan(step, start_carry, jnp.arange(heads_here * num_blocks, dtype=jnp...  42.5 us
    all_to_all x1, waiting for transfers between devices, shards(): lax.all_to_all(to_slots(grad_out), 'seq', split_axis=1, concat_axis=0, ti...  27.8 us
    all_to_all x1, waiting for transfers between devices, lax.all_to_all(jnp.stack(jnp.split(u_in, lax.psum(1, ax_name), axis=1)),...  23.7 us
    all_to_all x1, waiting for transfers between devices, shards(): lax.all_to_all(to_slots(outputs), 'seq', split_axis=1, concat_axis=0, til...  23.6 us
    all_to_all x1, blocking collectives, shards(): lax.all_to_all(grad_v_acc.reshape(total, 1, head_dim), 'seq', split_axis=...  21.5 us
  transfers between devices with their start and end apart: 8, of which 6 were waited for; matrix products, arithmetic and copies ran while one was open for 13% of the time, Pallas kernels for 0%

profile of v1, /device:TPU:0, one launch (start us, length us, event | category | flops | bytes accessed | tf_op | source)
XLA Modules:
  0.0 490.2 jit_solution(12479600725891654303)
XLA Ops:
  0.6 8.3 %all-to-all-start.2 = ((f32[128,16,4]{0,2,1:T(4,128)}), f32[128,16,4]{0,2,1:T(4,128)S(1)}, u32[]{:S(2)}, u32[]{:S(2)}) async-start(f32[128,16,4]{0,2,1:T(4,128)} %bitcast.216), calls=%async_computation.2 | async-start | bytes 65536 | tf_op jit(solution)/shard_map/all_to_all | solution.py:74
  9.0 3.2 copy.114
  21.8 7.2 %all-to-all-start.1 = ((bf16[128,16,128]{2,0,1:T(8,128)(2,1)}), bf16[128,16,128]{2,0,1:T(8,128)(2,1)S(1)}, u32[]{:S(2)}, u32[]{:S(2)}) async-start(bf16[128,16,128]{2,0,1:T(8,128)(2,1)} %bitcast.19), calls=%async_computation.1 | async-start | bytes 1048576 | tf_op jit(solution)/shard_map/all_to_all | solution.py:91
  31.0 8.9 %all-to-all-done.1 = bf16[128,16,128]{2,0,1:T(8,128)(2,1)S(1)} async-done(((bf16[128,16,128]{2,0,1:T(8,128)(2,1)}), bf16[128,16,128]{2,0,1:T(8,128)(2,1)S(1)}, u32[]{:S(2)}, u32[]{:S(2)}) %all-to-all-start.1) | async-done | bytes 524320 | tf_op jit(solution)/shard_map/all_to_all | solution.py:91
  39.9 3.7 all-to-all-start
  43.7 4.1 copy.122
  47.8 23.7 %all-to-all-done = bf16[16,128,1,512]{1,3,2,0:T(8,128)(2,1)S(1)} async-done(((bf16[16,128,1,512]{1,3,2,0:T(8,128)(2,1)}), bf16[16,128,1,512]{1,3,2,0:T(8,128)(2,1)S(1)}, u32[]{:S(2)}, u32[]{:S(2)}) %all-to-all-start) | async-done | bytes 2097184 | tf_op jit(solution)/shard_map/all_to_all | solution.py:10
  72.8 4.4 all-to-all-start.5
  77.3 4.1 copy.119
  81.3 23.6 %all-to-all-done.5 = bf16[128,16,512]{0,2,1:T(8,128)(2,1)} async-done(((bf16[128,16,512]{0,2,1:T(8,128)(2,1)}), bf16[128,16,512]{0,2,1:T(8,128)(2,1)}, u32[]{:S(2)}, u32[]{:S(2)}) %all-to-all-start.5) | async-done | bytes 2097184 | tf_op jit(solution)/shard_map/all_to_all | solution.py:71
  105.0 4.3 all-to-all-start.3
  109.4 27.8 %all-to-all-done.3 = bf16[128,16,512]{0,2,1:T(8,128)(2,1)S(1)} async-done(((bf16[128,16,512]{0,2,1:T(8,128)(2,1)}), bf16[128,16,512]{0,2,1:T(8,128)(2,1)S(1)}, u32[]{:S(2)}, u32[]{:S(2)}) %all-to-all-start.3) | async-done | bytes 2097184 | tf_op jit(solution)/shard_map/all_to_all | solution.py:72
  138.6 4.2 all-to-all-start.4
  143.1 4.3 copy.117
  147.4 4.2 reshape_reshape.3
  151.5 4.3 copy.123
  155.8 4.2 reshape.135
  160.0 4.3 copy.120
  164.3 4.2 reshape.130
  168.5 2.9 fusion.16
  173.0 235.0 %while.18 = (s32[]{:T(128)}, bf16[2048,4,128]{0,2,1:T(8,128)(2,1)}, f32[2048,128]{1,0:T(8,128)}, f32[2048,128]{1,0:T(8,128)S(1)}, s32[2048]{0:T(1024)S(1)}, /*in...) while((s32[]{:T(128)}, bf16[2048,4,128]{0,2,1:T(8,128)(2,1)}, ...), condition=%wide.region_3.4_spmd.clone.clone, body=%wide.region_2.3_spmd.clone.clone.sunk | while | flops 1354104832 | bytes 25862684 | solution.py:142
  176.5 2.6 exponential_select_fusion.2
  183.8 2.7 fusion.63
  190.8 2.6 exponential_select_fusion.2
  198.1 3.1 fusion.63
  205.5 2.5 exponential_select_fusion.2
  212.8 3.1 fusion.63
  220.2 2.5 exponential_select_fusion.2
  227.5 3.1 fusion.63
  235.0 2.5 exponential_select_fusion.2
  242.2 3.1 fusion.63
  249.7 2.5 exponential_select_fusion.2
  257.0 3.1 fusion.63
  264.4 2.5 exponential_select_fusion.2
  271.7 3.1 fusion.63
  279.1 2.5 exponential_select_fusion.2
  286.4 3.1 fusion.63
  293.8 2.5 exponential_select_fusion.2
  301.1 3.1 fusion.63
  308.5 2.5 exponential_select_fusion.2
  315.8 3.1 fusion.63
  323.2 2.5 exponential_select_fusion.2
  330.5 3.1 fusion.63
  337.9 2.5 exponential_select_fusion.2
  345.2 3.1 fusion.63
  352.6 2.5 exponential_select_fusion.2
  359.9 3.1 fusion.63
  367.4 2.5 exponential_select_fusion.2
  374.6 3.1 fusion.63
  382.1 2.5 exponential_select_fusion.2
  389.4 3.1 fusion.63
  396.8 2.5 exponential_select_fusion.2
  404.1 3.1 fusion.63
  408.0 21.5 %all_to_all.125 = f32[2048,1,128]{2,1,0:T(1,128)} all-to-all(f32[2048,1,128]{2,1,0:T(1,128)S(1)} %bitcast.184), channel_id=1, replica_groups=mesh['packs'=8,'seq'=16] {'seq'}, dimensions={0} | all-to-all | bytes 2097152 | tf_op jit(solution)/shard_map/all_to_all | solution.py:158
  429.5 4.0 all-to-all-start.7
  434.1 2.9 reduce.2
  437.0 2.9 copy.149
  439.9 2.8 reshape.151
  442.6 4.1 all-to-all-done.7
  446.8 3.7 all-to-all-start.6
  455.6 18.6 %all-to-all-done.6 = bf16[16,2,32768]{2,1,0:T(2,128)(2,1)S(1)} async-done(((bf16[16,2,32768]{2,1,0:T(2,128)(2,1)}), bf16[16,2,32768]{2,1,0:T(2,128)(2,1)S(1)}, u32[]{:S(2)}, u32[]{:S(2)}) %all-to-all-start.6) | async-done | bytes 2097184 | tf_op jit(solution)/shard_map/all_to_all | solution.py:146
  474.2 6.7 %reshape.152 = bf16[2048,1,512]{2,1,0:T(2,128)(2,1)} reshape(bf16[16,2,32768]{2,1,0:T(2,128)(2,1)S(1)} %all-to-all-done.6) | data formatting | bytes 4194304
  480.9 2.8 copy.144
  486.1 4.1 copy.131
  (211 shorter events, 126.4 us)
Async XLA Ops:
  0.6 8.3 %copy-start = (bf16[128,1024]{1,0:T(8,128)(2,1)S(1)}, bf16[128,1024]{1,0:T(8,128)(2,1)}, u32[]{:S(2)}) copy-start(bf16[128,1024]{1,0:T(8,128)(2,1)} %param.10) | copy-start | bytes 786436
  0.6 20.2 %all-to-all-start.2 = ((f32[128,16,4]{0,2,1:T(4,128)}), f32[128,16,4]{0,2,1:T(4,128)S(1)}, u32[]{:S(2)}, u32[]{:S(2)}) async-start(f32[128,16,4]{0,2,1:T(4,128)} %bitcast.216), calls=%async_computation.2 | async-start | bytes 65536 | tf_op jit(solution)/shard_map/all_to_all | solution.py:74
  21.8 18.2 %all-to-all-start.1 = ((bf16[128,16,128]{2,0,1:T(8,128)(2,1)}), bf16[128,16,128]{2,0,1:T(8,128)(2,1)S(1)}, u32[]{:S(2)}, u32[]{:S(2)}) async-start(bf16[128,16,128]{2,0,1:T(8,128)(2,1)} %bitcast.19), calls=%async_computation.1 | async-start | bytes 1048576 | tf_op jit(solution)/shard_map/all_to_all | solution.py:91
  39.9 31.6 %all-to-all-start = ((bf16[16,128,1,512]{1,3,2,0:T(8,128)(2,1)}), bf16[16,128,1,512]{1,3,2,0:T(8,128)(2,1)S(1)}, u32[]{:S(2)}, u32[]{:S(2)}) async-start(bf16[16,128,1,512]{1,3,2,0:T(8,128)(2,1)} %fusion.17), calls=%async_computation | async-start | bytes 4194304 | tf_op jit(solution)/shard_map/all_to_all | solution.py:10
  71.5 1.3 copy-start.2
  72.8 32.1 %all-to-all-start.5 = ((bf16[128,16,512]{0,2,1:T(8,128)(2,1)}), bf16[128,16,512]{0,2,1:T(8,128)(2,1)}, u32[]{:S(2)}, u32[]{:S(2)}) async-start(bf16[128,16,512]{0,2,1:T(8,128)(2,1)} %bitcast.205), calls=%async_computation.5 | async-start | bytes 4194304 | tf_op jit(solution)/shard_map/all_to_all | solution.py:71
  105.0 4.3 copy-start.5
  105.0 32.2 %all-to-all-start.3 = ((bf16[128,16,512]{0,2,1:T(8,128)(2,1)}), bf16[128,16,512]{0,2,1:T(8,128)(2,1)S(1)}, u32[]{:S(2)}, u32[]{:S(2)}) async-start(bf16[128,16,512]{0,2,1:T(8,128)(2,1)} %bitcast.206), calls=%async_computation.3 | async-start | bytes 4194304 | tf_op jit(solution)/shard_map/all_to_all | solution.py:72
  109.3 33.5 %copy-start.6 = (s32[8]{0:T(128)S(1)}, s32[8]{0:T(128)}, u32[]{:S(2)}) copy-start(s32[8]{0:T(128)} %param.15) | copy-start | bytes 100
  137.1 1.5 copy-start.3
  138.6 32.8 %all-to-all-start.4 = ((bf16[128,16,128]{2,0,1:T(8,128)(2,1)}), bf16[128,16,128]{2,0,1:T(8,128)(2,1)S(1)}, u32[]{:S(2)}, u32[]{:S(2)}) async-start(bf16[128,16,128]{2,0,1:T(8,128)(2,1)} %bitcast.30), calls=%async_computation.4 | async-start | bytes 1048576 | tf_op jit(solution)/shard_map/all_to_all | solution.py:92
  429.5 4.5 copy-start.4
  429.5 17.2 %all-to-all-start.7 = ((f32[2048,1,128]{2,1,0:T(1,128)}), f32[2048,1,128]{2,1,0:T(1,128)S(1)}, u32[]{:S(2)}, u32[]{:S(2)}) async-start(f32[2048,1,128]{2,1,0:T(1,128)} %bitcast.40), calls=%async_computation.7 | async-start | bytes 2097152 | tf_op jit(solution)/shard_map/all_to_all | solution.py:155
  446.8 27.4 %all-to-all-start.6 = ((bf16[16,2,32768]{2,1,0:T(2,128)(2,1)}), bf16[16,2,32768]{2,1,0:T(2,128)(2,1)S(1)}, u32[]{:S(2)}, u32[]{:S(2)}) async-start(bf16[16,2,32768]{2,1,0:T(2,128)(2,1)} %reshape.151), calls=%async_computation.6 | async-start | bytes 4194304 | tf_op jit(solution)/shard_map/all_to_all | solution.py:146
  486.1 4.1 copy-start.1
